TPU v7x, 32 devices: a whole 2x2x4 slice. The times are simulated.
32 devices in a mesh: blk: 4 (over y, x), rep: 8 (over z, core).
Axes of the slice: x: 2, y: 2, z: 4, core: 2. Of those that a mesh axis runs over, the one named last changes fastest.
Arguments:
- query_hidden: bfloat16 [8, 16, 32, 768], P('rep', 'blk'), may hold values from -18 to 18
- passage_hidden: bfloat16 [8, 16, 512, 768], P('rep', 'blk'), may hold values from -6 to 6
- lengths: int32 [8, 16], P('rep', 'blk'), may hold values from 64 to 512
- projection: bfloat16 [768, 128], replicated, may hold values from -0.21875 to 0.21875
Outputs:
- query_grad: float32 [8, 16, 32, 128], P('rep', 'blk')
- passage_grad: float32 [8, 16, 512, 128], P('rep', 'blk')
- grad_weight: float32 [768, 128], replicated
- loss: float32 [], replicated
All inputs are finite; a program needn't handle non-finite values.
Results may differ from a plain program's by a relative error of at most 0.0097.
Values may be sent and summed in bfloat16 or wider, within the bound.
A program may use at most 128 MiB of HBM per device.

v0:
```python
import jax
import jax.numpy as jnp
from jax import lax
from jax.sharding import PartitionSpec as P

temper = 0.5


def soft_scores(scores, lens):
    slots = scores.shape[-1]
    valid = lax.broadcasted_iota(jnp.int32, (lens.shape[0], slots), 1) < lens[:, None]
    scaled = jnp.where(valid[None], scores / temper, -jnp.inf)
    top = jnp.max(scaled, -1, keepdims=True)
    logz = top + jnp.log(jnp.sum(jnp.exp(scaled - top), -1, keepdims=True))
    pooled = temper * (logz[..., 0] - jnp.log(lens.astype(jnp.float32))[None])
    return (pooled, scaled, logz)


def cross_entropy(score, first, total):
    top = jnp.max(score, 1, keepdims=True)
    lse = top + jnp.log(jnp.sum(jnp.exp(score - top), 1, keepdims=True))
    target = lax.broadcasted_iota(jnp.int32, score.shape, 1) == first + lax.broadcasted_iota(
        jnp.int32, score.shape, 0
    )
    loss_part = jnp.sum(lse[:, 0] - jnp.sum(jnp.where(target, score, 0.0), 1))
    dscore = (jnp.exp(score - lse) - target.astype(jnp.float32)) / total
    return (loss_part, dscore)


def weighted(dscore, scaled, logz, qlen):
    spread = jnp.repeat(dscore, qlen, axis=0)
    grad_a = (spread[:, :, None] * jnp.exp(scaled - logz)).astype(jnp.bfloat16)
    return grad_a.reshape(grad_a.shape[0], -1)


def shards(query_hidden, passage_hidden, lengths, projection):
    hidden = projection.shape[0]
    nquery = query_hidden.shape[1]
    qlen = query_hidden.shape[2]
    npass = passage_hidden.shape[1]
    plen = passage_hidden.shape[2]
    groups = lax.axis_size("blk")
    total = groups * lax.axis_size("rep") * nquery
    first = lax.axis_index("blk") * nquery
    qflat = query_hidden[0].reshape(-1, hidden)
    pflat = passage_hidden[0].reshape(-1, hidden)
    qtok = jnp.dot(qflat, projection, preferred_element_type=jnp.float32).astype(jnp.bfloat16)
    ptok = jnp.dot(pflat, projection, preferred_element_type=jnp.float32).astype(jnp.bfloat16)
    every_tok = lax.all_gather(qtok, "blk", axis=0, tiled=True)
    scores = jnp.dot(every_tok, ptok.T, preferred_element_type=jnp.float32).reshape(
        groups * nquery * qlen, npass, plen
    )
    pooled, scaled, logz = soft_scores(scores, lengths[0])
    block_score = jnp.sum(pooled.reshape(groups * nquery, qlen, npass), 1)
    score = lax.all_to_all(block_score, "blk", split_axis=0, concat_axis=1, tiled=True)
    loss_part, dscore = cross_entropy(score, first, total)
    block_grad = lax.all_to_all(dscore, "blk", split_axis=1, concat_axis=0, tiled=True)
    grad_a = weighted(block_grad, scaled, logz, qlen)
    pgrad = jnp.dot(grad_a.T, every_tok, preferred_element_type=jnp.float32)
    qgrad = lax.psum_scatter(
        jnp.dot(grad_a, ptok, preferred_element_type=jnp.float32),
        "blk",
        scatter_dimension=0,
        tiled=True,
    )
    wgrad = jnp.dot(qflat.T, qgrad.astype(jnp.bfloat16), preferred_element_type=jnp.float32)
    wgrad = wgrad + jnp.dot(pflat.T, pgrad.astype(jnp.bfloat16), preferred_element_type=jnp.float32)
    wgrad, loss_sum = lax.psum((wgrad, loss_part), ("blk", "rep"))
    query_grad = qgrad.reshape(1, nquery, qlen, -1)
    passage_grad = pgrad.reshape(1, npass, plen, -1)
    return (query_grad, passage_grad, wgrad, loss_sum / total)


def solution(mesh):
    return jax.shard_map(
        shards,
        mesh=mesh,
        in_specs=(P("rep", "blk", None, None), P("rep", "blk", None, None), P("rep", "blk"), P()),
        out_specs=(P("rep", "blk", None, None), P("rep", "blk", None, None), P(), P()),
        check_vma=False,
    )
```

profile of v0, /device:TPU:0, one launch (start us, length us, event | category | flops | bytes accessed | tf_op | source)
XLA Modules:
  0.0 233.2 jit_solution(2799079594073589666)
XLA Ops:
  7.2 0.0 copy-start
  7.2 0.0 copy-start.9
  7.2 1.9 copy-done
  9.1 1.9 convolution_convert_fusion
  11.0 0.0 copy-start.6
  11.0 0.2 convolution_convert_fusion.1
  11.2 9.9 %all_gather.3 = bf16[512,128]{1,0:T(8,128)(2,1)S(1)} all-gather(bf16[128,128]{1,0:T(8,128)(2,1)S(1)} %convolution_convert_fusion.1), channel_id=1, replica_groups=mesh['blk'=4,'rep'=8] {'blk'}, dimensions={0}, use_global_device_ids=true | all-gather | bytes 163840 | tf_op jit(solution)/shard_map/all_gather | solution.py:49
  21.2 2.6 %convolution_multiply_fusion = f32[512,2048]{1,0:T(8,128)} fusion(bf16[512,128]{1,0:T(8,128)(2,1)S(1)} %all_gather.3, bf16[2048,128]{1,0:T(8,128)(2,1)S(1)} %convolution_convert_fusion), kind=kOutput, calls=%fused_computation.3 | convolution fusion | flops 269484032 | bytes 4849664 | tf_op jit(solution)/shard_map/dot_general | solution.py:50
  23.8 6.0 %div.19 = f32[512,4,512]{2,1,0:T(4,128)} reshape(f32[512,2048]{1,0:T(8,128)} %convolution_multiply_fusion) | data formatting | bytes 8388608 | tf_op jit(solution)/shard_map/div | solution.py:12
  29.8 0.1 iota_compare_fusion
  29.9 3.3 %select_reduce_fusion = f32[512,4]{1,0:T(8,128)S(1)} fusion(f32[512,4,512]{2,1,0:T(4,128)} %div.19, pred[4,512]{1,0:T(4,128)(4,1)S(1)} %iota_compare_fusion), kind=kLoop, calls=%fused_computation.2 | loop fusion | flops 2095104 | bytes 4204544 | tf_op jit(solution)/shard_map/reduce_max | solution.py:13
  33.2 0.1 copy-done.1
  33.3 2.6 %exponential_reduce_fusion = f32[512,4]{1,0:T(8,128)S(1)} fusion(f32[512,4,512]{2,1,0:T(4,128)S(1)} %copy-done.1, f32[512,4]{1,0:T(8,128)S(1)} %select_reduce_fusion, pred[4,512]{1,0:T(4,128)(4,1)S(1)} %iota_compare_fusion), kind=kLoop, calls=%fused_computation.1 | loop fusion | flops 3143680 | bytes 4212736 | tf_op jit(solution)/shard_map/reduce_sum | solution.py:14
  35.9 0.1 multiply_reduce_fusion
  36.0 0.7 copy.11
  36.7 3.2 %all-to-all-start = ((f32[4,4,4]{1,2,0:T(4,128)}), f32[4,4,4]{1,2,0:T(4,128)S(1)}, u32[]{:S(2)}, u32[]{:S(2)}) async-start(f32[4,4,4]{1,2,0:T(4,128)} %copy.11), calls=%async_computation | async-start | bytes 16384 | tf_op jit(solution)/shard_map/all_to_all | solution.py:55
  40.0 0.6 multiply_add_fusion
  40.5 0.5 iota_add_fusion
  41.1 0.7 sub.65
  41.8 0.0 copy-start.10
  41.8 0.0 copy-start.12
  41.8 3.9 %copy.21 = f32[64,8,4,512]{3,1,2,0:T(8,128)} copy(f32[64,8,4,512]{3,2,1,0:T(4,128)S(1)} %bitcast.49) | data formatting | bytes 8388608
  45.8 0.1 fusion.6
  45.8 0.6 subtract_reduce_fusion
  46.5 0.7 fusion.5
  47.1 4.2 %all-to-all-start.1 = ((f32[4,4,4]{0,2,1:T(4,128)}), f32[4,4,4]{0,2,1:T(4,128)S(1)}, u32[]{:S(2)}, u32[]{:S(2)}) async-start(f32[4,4,4]{0,2,1:T(4,128)} %fusion.5), calls=%async_computation.1 | async-start | bytes 16384 | tf_op jit(solution)/shard_map/all_to_all | solution.py:57
  51.3 0.1 lt.24
  51.4 4.6 %all-to-all-done.1 = f32[4,4,4]{0,2,1:T(4,128)S(1)} async-done(((f32[4,4,4]{0,2,1:T(4,128)}), f32[4,4,4]{0,2,1:T(4,128)S(1)}, u32[]{:S(2)}, u32[]{:S(2)}) %all-to-all-start.1) | async-done | bytes 288 | tf_op jit(solution)/shard_map/all_to_all | solution.py:57
  56.0 0.1 copy.17
  56.1 0.7 mul.27
  56.9 2.0 copy.19
  58.9 0.1 copy-done.2
  59.0 1.3 copy-done.4
  60.3 1.6 multiply_convert_fusion
  61.9 1.3 copy-done.3
  63.2 1.4 fusion.10
  64.6 0.0 reduce-scatter.2.cloned.1.call-update
  64.7 0.0 all-reduce.2.cloned.1.call-start
  64.7 2.3 fusion.11
  67.0 0.0 copy-start.5
  67.0 1.0 copy-done.5
  68.0 0.6 fusion.1
  68.6 19.9 %reduce-scatter.2.cloned.1.call-done = f32[128,128]{1,0:T(8,128)} async-done(((f32[512,128]{1,0:T(8,128)}), f32[128,128]{1,0:T(8,128)}) %reduce-scatter.2.cloned.1.call-update) | async-done | bytes 65552 | tf_op jit(solution)/shard_map/reduce_scatter | solution.py:60
  88.5 1.9 fusion
  90.5 0.0 all-reduce.2.cloned.1.call-update
  90.5 39.6 %psum.15 = f32[]{:T(128)} all-reduce(f32[]{:T(128)} %get-tuple-element.14), channel_id=1, replica_groups=mesh['blk'=4,'rep'=8] {'blk','rep'}, use_global_device_ids=true, to_apply=%region_9.10 | all-reduce | flops 1 | bytes 8 | tf_op jit(solution)/shard_map/psum | solution.py:68
  130.7 92.6 %all-reduce.2.cloned.1.call-done = f32[768,128]{0,1:T(8,128)} async-done(((f32[768,128]{0,1:T(8,128)}), f32[768,128]{0,1:T(8,128)}) %all-reduce.2.cloned.1.call-update) | async-done | bytes 393232 | tf_op jit(solution)/shard_map/psum | solution.py:68
  223.3 1.9 copy.14
  (24 shorter events, 0.1 us)
Async XLA Ops:
  7.2 1.9 copy-start
  7.2 3.8 %copy-start.8 = (bf16[768,128]{1,0:T(8,128)(2,1)S(1)}, bf16[768,128]{1,0:T(8,128)(2,1)}, u32[]{:S(2)}) copy-start(bf16[768,128]{1,0:T(8,128)(2,1)} %param.7) | copy-start | bytes 589828
  7.2 3.8 %copy-start.9 = (bf16[1,4,32,768]{3,2,1,0:T(8,128)(2,1)S(1)}, bf16[1,4,32,768]{3,2,1,0:T(8,128)(2,1)}, u32[]{:S(2)}) copy-start(bf16[1,4,32,768]{3,2,1,0:T(8,128)(2,1)} %param.4) | copy-start | bytes 589828
  11.0 10.2 %copy-start.6 = (bf16[2048,128]{1,0:T(8,128)(2,1)}, bf16[2048,128]{1,0:T(8,128)(2,1)S(1)}, u32[]{:S(2)}) copy-start(bf16[2048,128]{1,0:T(8,128)(2,1)S(1)} %convolution_convert_fusion) | copy-start | bytes 1572868
  23.8 6.0 %copy-start.11 = (s32[1,4]{1,0:T(1,128)S(1)}, s32[1,4]{1,0:T(1,128)}, u32[]{:S(2)}) copy-start(s32[1,4]{1,0:T(1,128)} %param.6) | copy-start | bytes 52
  29.8 3.4 %copy-start.1 = (f32[512,4,512]{2,1,0:T(4,128)S(1)}, f32[512,4,512]{2,1,0:T(4,128)}, u32[]{:S(2)}) copy-start(f32[512,4,512]{2,1,0:T(4,128)} %div.19) | copy-start | bytes 12582916
  36.7 9.0 %all-to-all-start = ((f32[4,4,4]{1,2,0:T(4,128)}), f32[4,4,4]{1,2,0:T(4,128)S(1)}, u32[]{:S(2)}, u32[]{:S(2)}) async-start(f32[4,4,4]{1,2,0:T(4,128)} %copy.11), calls=%async_computation | async-start | bytes 16384 | tf_op jit(solution)/shard_map/all_to_all | solution.py:55
  41.8 4.0 %copy-start.10 = (s32[4,4]{1,0:T(4,128)S(1)}, s32[4,4]{1,0:T(4,128)}, u32[]{:S(2)}) copy-start(s32[4,4]{1,0:T(4,128)} %multiply_add_fusion) | copy-start | bytes 196
  41.8 4.0 %copy-start.13 = (s32[4]{0:T(128)S(1)}, s32[4]{0:T(128)}, u32[]{:S(2)}) copy-start(s32[4]{0:T(128)} %iota_add_fusion) | copy-start | bytes 52
  41.8 9.5 %copy-start.12 = (s32[1,4]{1,0:T(1,128)S(1)}, s32[1,4]{1,0:T(1,128)}, u32[]{:S(2)}) copy-start(s32[1,4]{1,0:T(1,128)} %param.6) | copy-start | bytes 52
  47.1 8.8 %all-to-all-start.1 = ((f32[4,4,4]{0,2,1:T(4,128)}), f32[4,4,4]{0,2,1:T(4,128)S(1)}, u32[]{:S(2)}, u32[]{:S(2)}) async-start(f32[4,4,4]{0,2,1:T(4,128)} %fusion.5), calls=%async_computation.1 | async-start | bytes 16384 | tf_op jit(solution)/shard_map/all_to_all | solution.py:57
  51.3 37.2 %reduce-scatter.2.cloned.1.call-start = ((), (), s32[]{:S(2)}) async-start(), calls=%async_computation.3 | async-start | bytes 327680 | tf_op jit(solution)/shard_map/reduce_scatter | solution.py:60
  56.8 2.2 copy-start.2
  56.8 3.5 %copy-start.4 = (f32[64,8,4,512]{3,1,2,0:T(8,128)S(1)}, f32[64,8,4,512]{3,1,2,0:T(8,128)}, u32[]{:S(2)}) copy-start(f32[64,8,4,512]{3,1,2,0:T(8,128)} %copy.21) | copy-start | bytes 12582916
  60.3 2.9 %copy-start.7 = (bf16[2048,128]{1,0:T(8,128)(2,1)S(1)}, bf16[2048,128]{1,0:T(8,128)(2,1)}, u32[]{:S(2)}) copy-start(bf16[2048,128]{1,0:T(8,128)(2,1)} %copy-done.6) | copy-start | bytes 1572868
  61.9 1.4 copy-start.3
  64.7 158.7 %all-reduce.2.cloned.1.call-start = ((), (), s32[]{:S(2)}) async-start(), calls=%async_computation.4 | async-start | bytes 786432 | tf_op jit(solution)/shard_map/psum | solution.py:68
  67.0 1.0 copy-start.5
Sparse Core Ops, SparseCore 0:
  64.8 23.6 reduce-scatter.1
  94.4 128.9 all-reduce.1
where the time goes:
time: 234 us; the launch traced here: 233 us
  waiting for transfers between devices  117 us (50%)
  blocking collectives  49.5 us (21%)
  local copies, waits for them, and re-layouts  21.9 us (9%)
  between operations  16 us (7%)
  matrix products  11 us (5%)
  other arithmetic  10.1 us (4%)
  starting transfers between devices  7.45 us (3%)
    psum x1, waiting for transfers between devices, shards(): wgrad, loss_sum = lax.psum((wgrad, loss_part), ('blk', 'rep'))  92.6 us
    psum x1, blocking collectives, shards(): wgrad, loss_sum = lax.psum((wgrad, loss_part), ('blk', 'rep'))  39.6 us
    reduce_scatter x1, waiting for transfers between devices, shards(): lax.psum_scatter(jnp.dot(grad_a, ptok, preferred_element_type=jnp.float32...  19.9 us
    unnamed x33, local copies, waits for them, and re-layouts  13.6 us
    all_gather x1, blocking collectives, shards(): every_tok = lax.all_gather(qtok, 'blk', axis=0, tiled=True)  9.94 us
    div x1, local copies, waits for them, and re-layouts, soft_scores(): scaled = jnp.where(valid[None], scores / temper, -jnp.inf)  6.03 us
  transfers between devices with their start and end apart: 4, of which 3 were waited for; matrix products, arithmetic and copies ran while one was open for 4% of the time, Pallas kernels for 0%

commit v1 on v0

v1 whole, which is shorter than its diff:
```python
import functools

import jax
import jax.numpy as jnp
from jax import lax
from jax.experimental import pallas as pl
from jax.experimental.pallas import tpu as pltpu
from jax.sharding import PartitionSpec as P

MESH = pl.DeviceIdType.MESH
F32 = jnp.float32
BF16 = jnp.bfloat16
HIGH = lax.Precision.HIGHEST
NT = (((1,), (1,)), ((), ()))

temper = 0.5


def rows_iota(shape, dim):
    return lax.broadcasted_iota(jnp.int32, shape, dim)


def kernel(
    dims, lens, qhid, proj, phid, qg_out, pg_out, wg_out, loss_out,
    tok, ptok, ptok_t, phid_v, expo, grad_a, sums, pooled, sc, lo, qsend, qrecv, pg_v, pg_t,
    wsend, wrecv, zbuf, cbuf,
    in_sem, out_sem, tok_s, tok_r, sc_s, sc_r, lo_s, lo_r, qg_s, qg_r, ws_s, ws_r, z_s, z_r, c_s, c_r,
):
    nblk, nrep, ncore, nquery, qlen, npass, plen = dims
    ntok = nquery * qlen
    nqi = nblk * ntok
    nq_all = nblk * nquery
    nz = nrep // ncore
    na = nblk * ncore
    dim = proj.shape[1]
    total = nq_all * nrep
    blk = lax.axis_index("blk")
    rep = lax.axis_index("rep")
    core = lax.rem(rep, ncore)
    zed = rep // ncore
    me_a = blk * ncore + core

    def blk_peer(k):
        return (lax.rem(blk + k, nblk), rep)

    def rep_peer(k):
        return (blk, lax.rem(rep + k, nrep))

    def a_index(k):
        return lax.rem(me_a + k, na)

    def a_peer(k):
        other = a_index(k)
        return (other // ncore, zed * ncore + lax.rem(other, ncore))

    def z_peer(k):
        return (blk, lax.rem(zed + k, nz) * ncore + core)

    def share(src, dst, send, recv, peer, count):
        copies = []
        for k in range(1, count):
            copy = pltpu.make_async_remote_copy(
                src_ref=src(k), dst_ref=dst, send_sem=send.at[k - 1], recv_sem=recv.at[k - 1],
                device_id=peer(k), device_id_type=MESH,
            )
            copy.start()
            copies.append(copy)
        return copies

    loads = []
    for p in range(npass):
        load = pltpu.make_async_copy(phid.at[p], phid_v.at[p], in_sem.at[p])
        load.start()
        loads.append(load)

    barrier = pltpu.get_barrier_semaphore()
    greeted = 0
    for count, peer in ((na, a_peer), (nrep, rep_peer)):
        for k in range(1, count):
            pl.semaphore_signal(barrier, inc=1, device_id=peer(k), device_id_type=MESH)
            greeted += 1

    tok[blk] = jnp.dot(qhid[...], proj[...], preferred_element_type=F32).astype(BF16)
    pl.semaphore_wait(barrier, greeted)
    tok_copies = share(lambda k: tok.at[blk], tok.at[blk], tok_s, tok_r, blk_peer, nblk)

    pooled[...] = jnp.zeros_like(pooled)
    sums[...] = jnp.ones_like(sums)
    for p in range(npass):
        loads[p].wait()
        vec = jnp.dot(phid_v[p], proj[...], preferred_element_type=F32).astype(BF16)
        ptok[p] = vec
        ptok_t[p] = vec.T
    for copy in tok_copies:
        copy.wait_recv()
    every = tok[...].reshape(nqi, dim)

    def forward(p, carry):
        count = lens[0, p]
        a = lax.dot_general(ptok[p], every, NT, preferred_element_type=F32)
        valid = rows_iota(a.shape, 0) < count
        scaled = jnp.where(valid, a / temper, -jnp.inf)
        top = jnp.max(scaled, 0, keepdims=True)
        e = jnp.exp(scaled - top)
        expo[p] = e
        s = jnp.sum(e, 0, keepdims=True)
        sums[pl.ds(p, 1), :] = s
        size = jnp.log(jnp.full((1, nqi), count, jnp.int32).astype(F32))
        pooled[pl.ds(p, 1), :] = temper * (top + jnp.log(s) - size)
        return carry

    lax.fori_loop(0, npass, forward, 0)

    ppad = pooled.shape[0]
    qpad = sc.shape[2]
    owner = rows_iota((nqi, qpad), 1) * qlen
    token = rows_iota((nqi, qpad), 0)
    pick = ((token >= owner) & (token < owner + qlen)).astype(F32)
    own = jnp.dot(pooled[...], pick, precision=HIGH, preferred_element_type=F32)
    sc[blk] = own
    sc_copies = share(lambda k: sc.at[blk], sc.at[blk], sc_s, sc_r, blk_peer, nblk)
    owner_t = rows_iota((qpad, nqi), 0) * qlen
    token_t = rows_iota((qpad, nqi), 1)
    spread = ((token_t >= owner_t) & (token_t < owner_t + qlen)).astype(F32)
    inv = 1.0 / sums[...]
    for copy in sc_copies:
        copy.wait_recv()

    score = sc[...]
    row = rows_iota(score.shape, 1)
    lane = rows_iota(score.shape, 2)
    slot = rows_iota(score.shape, 0)
    live = row < npass
    hidden_score = jnp.where(live, score, -jnp.inf)
    top = jnp.max(jnp.max(hidden_score, 0), 0, keepdims=True)
    lse = top + jnp.log(jnp.sum(jnp.sum(jnp.exp(hidden_score - top[None]), 0), 0, keepdims=True))
    hit = live & (slot * npass + row == lane)
    aim = jnp.sum(jnp.sum(jnp.where(hit, score, 0.0), 0), 0, keepdims=True)
    gap = jnp.where(rows_iota(lse.shape, 1) < nq_all, lse - aim, 0.0)
    part = jnp.sum(gap, 1, keepdims=True)
    lo[rep] = jnp.broadcast_to(part, lo.shape[1:])
    lo_copies = share(lambda k: lo.at[rep], lo.at[rep], lo_s, lo_r, rep_peer, nrep)

    mine = rows_iota(own.shape, 0) + blk * npass == rows_iota(own.shape, 1)
    dscore = (jnp.exp(own - lse) - mine.astype(F32)) / total
    factor = jnp.dot(dscore, spread, precision=HIGH, preferred_element_type=F32) * inv
    sums[...] = factor

    def backward(p, acc):
        d = (expo[p] * sums[pl.ds(p, 1), :]).astype(BF16)
        grad_a[p] = d
        return acc + jnp.dot(ptok_t[p], d, preferred_element_type=F32)

    qg_t = lax.fori_loop(0, npass, backward, jnp.zeros((dim, nqi), F32))
    for b in range(nblk):
        qsend[b] = qg_t[:, b * ntok : (b + 1) * ntok]
    qrecv[blk] = qsend[blk]
    qg_copies = share(lambda k: qsend.at[lax.rem(blk + k, nblk)], qrecv.at[blk], qg_s, qg_r, blk_peer, nblk)

    def passages(p, acc):
        g = jnp.dot(grad_a[p], every, preferred_element_type=F32)
        pg_v[p] = g
        return acc + jnp.dot(g.astype(BF16).T, phid_v[p], preferred_element_type=F32)

    wg_t = lax.fori_loop(0, npass, passages, jnp.zeros((dim, qhid.shape[1]), F32))
    store = pltpu.make_async_copy(pg_v, pg_out, out_sem)
    store.start()
    for copy in qg_copies:
        copy.wait_recv()
    mine_t = jnp.sum(qrecv[...], 0)
    wg_t = wg_t + jnp.dot(mine_t.astype(BF16), qhid[...], preferred_element_type=F32)
    depth = dim // na
    for a in range(na):
        wsend[a] = wg_t[a * depth : (a + 1) * depth].astype(BF16)
    wrecv[me_a] = wsend[me_a]
    ws_copies = share(lambda k: wsend.at[a_index(k)], wrecv.at[me_a], ws_s, ws_r, a_peer, na)
    qg_out[...] = mine_t.T
    for copy in ws_copies:
        copy.wait_recv()
    zbuf[zed] = jnp.sum(wrecv[...].astype(F32), 0).astype(BF16)
    z_copies = share(lambda k: zbuf.at[zed], zbuf.at[zed], z_s, z_r, z_peer, nz)
    for copy in lo_copies:
        copy.wait_recv()
    loss_out[...] = jnp.sum(lo[...], 0) / total
    for copy in z_copies:
        copy.wait_recv()
    cbuf[me_a] = jnp.sum(zbuf[...].astype(F32), 0).astype(BF16)
    c_copies = share(lambda k: cbuf.at[me_a], cbuf.at[me_a], c_s, c_r, a_peer, na)
    for copy in tok_copies + sc_copies + lo_copies + qg_copies + ws_copies + z_copies:
        copy.wait_send()
    store.wait()
    for copy in c_copies:
        copy.wait_recv()
    for a in range(na):
        wg_out[a * depth : (a + 1) * depth, :] = cbuf[a].astype(F32)
    for copy in c_copies:
        copy.wait_send()


def shards(query_hidden, passage_hidden, lengths, projection):
    hidden, dim = projection.shape
    nquery, qlen = query_hidden.shape[1:3]
    npass, plen = passage_hidden.shape[1:3]
    nblk = lax.axis_size("blk")
    nrep = lax.axis_size("rep")
    ncore = 2 if nrep % 2 == 0 else 1
    nz = nrep // ncore
    na = nblk * ncore
    ntok = nquery * qlen
    nqi = nblk * ntok
    ppad = -(-npass // 8) * 8
    qpad = -(-nblk * nquery // 128) * 128
    dims = (nblk, nrep, ncore, nquery, qlen, npass, plen)
    vmem = pl.BlockSpec(memory_space=pltpu.VMEM)
    sem = lambda n: pltpu.SemaphoreType.DMA((max(n, 1),))
    pairs = []
    for n in (nblk, nblk, nrep, nblk, na, nz, na):
        pairs += [sem(n - 1), sem(n - 1)]
    qg, pg, wg_t, loss = pl.pallas_call(
        functools.partial(kernel, dims),
        out_shape=(
            jax.ShapeDtypeStruct((ntok, dim), F32),
            jax.ShapeDtypeStruct((npass, plen, dim), F32),
            jax.ShapeDtypeStruct((dim, hidden), F32),
            jax.ShapeDtypeStruct((8, 128), F32),
        ),
        in_specs=[
            pl.BlockSpec(memory_space=pltpu.SMEM), vmem, vmem, pl.BlockSpec(memory_space=pl.ANY),
        ],
        out_specs=(vmem, pl.BlockSpec(memory_space=pl.ANY), vmem, vmem),
        scratch_shapes=[
            pltpu.VMEM((nblk, ntok, dim), BF16),
            pltpu.VMEM((npass, plen, dim), BF16),
            pltpu.VMEM((npass, dim, plen), BF16),
            pltpu.VMEM((npass, plen, hidden), BF16),
            pltpu.VMEM((npass, plen, nqi), F32),
            pltpu.VMEM((npass, plen, nqi), BF16),
            pltpu.VMEM((ppad, nqi), F32),
            pltpu.VMEM((ppad, nqi), F32),
            pltpu.VMEM((nblk, ppad, qpad), F32),
            pltpu.VMEM((nrep, 8, 128), F32),
            pltpu.VMEM((nblk, dim, ntok), F32),
            pltpu.VMEM((nblk, dim, ntok), F32),
            pltpu.VMEM((npass, plen, dim), F32),
            pltpu.VMEM((dim, plen), BF16),
            pltpu.VMEM((na, dim // na, hidden), BF16),
            pltpu.VMEM((na, dim // na, hidden), BF16),
            pltpu.VMEM((nz, dim // na, hidden), BF16),
            pltpu.VMEM((na, dim // na, hidden), BF16),
            sem(npass),
            pltpu.SemaphoreType.DMA,
        ] + pairs,
        compiler_params=pltpu.CompilerParams(
            collective_id=0, has_side_effects=True, vmem_limit_bytes=56 << 20
        ),
    )(
        lengths,
        query_hidden.reshape(ntok, hidden),
        projection,
        passage_hidden.reshape(npass, plen, hidden),
    )
    return (
        qg.reshape(1, nquery, qlen, dim),
        pg.reshape(1, npass, plen, dim),
        wg_t.T,
        loss[0, 0],
    )


def solution(mesh):
    return jax.shard_map(
        shards,
        mesh=mesh,
        in_specs=(P("rep", "blk", None, None), P("rep", "blk", None, None), P("rep", "blk"), P()),
        out_specs=(P("rep", "blk", None, None), P("rep", "blk", None, None), P(), P()),
        check_vma=False,
    )
```

time: 234 us -> 42 us (0.18)
  waiting for transfers between devices: 117 us -> 0 us
  blocking collectives: 49.5 us -> 0 us
  Pallas kernels: 0 us -> 34.2 us
  between operations: 16 us -> 0.64 us
  local copies, waits for them, and re-layouts: 21.9 us -> 6.83 us
  matrix products: 11 us -> 0 us
  other arithmetic: 10.1 us -> 0 us
  starting transfers between devices: 7.45 us -> 0 us
    psum x1 -> x0, waiting for transfers between devices: 92.6 us -> none  [shards(): wgrad, loss_sum = lax.psum((wgrad, loss_part), ('blk', 'rep'))]
    psum x1 -> x0, blocking collectives: 39.6 us -> none  [shards(): wgrad, loss_sum = lax.psum((wgrad, loss_part), ('blk', 'rep'))]
    pallas_call x0 -> x1, Pallas kernels: none -> 34.2 us  [shards(): pl.pallas_call(functools.partial(kernel, dims), out_shape=(jax.ShapeDtype...]
    reduce_scatter x1 -> x0, waiting for transfers between devices: 19.9 us -> none  [shards(): lax.psum_scatter(jnp.dot(grad_a, ptok, preferred_element_type=jnp.float32...]
    dot_general x7 -> x0, matrix products: 11 us -> none  [the longest x1 2.64 us: shards(): jnp.dot(every_tok, ptok.T, preferred_element_type=jnp.float32)]
    all_gather x1 -> x0, blocking collectives: 9.94 us -> none  [shards(): every_tok = lax.all_gather(qtok, 'blk', axis=0, tiled=True)]
    unnamed x33 -> x3, local copies, waits for them, and re-layouts: 13.6 us -> 5.64 us
    all_to_all x2 -> x0, starting transfers between devices: 7.4 us -> none  [the longest x1 4.15 us: shards(): lax.all_to_all(dscore, 'blk', split_axis=1, concat_axis=0, tiled=True)]
  transfers between devices with their start and end apart: 4 -> 0, of which waited for: 3 -> 0; matrix products, arithmetic and copies ran while one was open for 4% -> 0% of each run, Pallas kernels for 0% -> 0%
where the time goes in v1:
time: 42 us; the launch traced here: 41.7 us
  Pallas kernels  34.2 us (81%)
  local copies, waits for them, and re-layouts  6.83 us (16%)
  between operations  0.64 us (2%)
    pallas_call x1, Pallas kernels, shards(): pl.pallas_call(functools.partial(kernel, dims), out_shape=(jax.ShapeDtype...  34.2 us
    unnamed x3, local copies, waits for them, and re-layouts  5.64 us
    slice x1, local copies, waits for them, and re-layouts, shards(): loss[0, 0]  1.18 us

profile of v1, /device:TPU:0, one launch (start us, length us, event | category | flops | bytes accessed | tf_op | source)
XLA Modules:
  0.0 41.7 jit_solution(11947530131417892497)
XLA Ops:
  0.6 34.2 %shard_map.75 = (f32[128,128]{1,0:T(8,128)}, f32[4,512,128]{2,1,0:T(8,128)}, f32[128,768]{1,0:T(8,128)}, f32[8,128]{1,0:T(8,128)}) custom-call(s32[1,4]{1,0:T(1,128)} %lens.1, bf16[128,768]{1,0:T(8,128)(2,1)} %bitcast.9, bf16[768,128]{1,0:T(8,128)(2,1)} %proj.1, bf16[4,512,768]{2,1,0:T(8,128)(2,1)} %bitcast.6), custom_call_target="tpu_custom_call" | custom-call | tf_op jit(solution)/shard_map/pallas_call | solution.py:219
  34.8 1.2 %slice.3 = f32[1,1]{1,0:T(1,128)} slice(f32[8,128]{1,0:T(8,128)} %get-tuple-element.11), slice={[0:1], [0:1]} | slice | bytes 8 | tf_op jit(solution)/shard_map/slice | solution.py:266
  36.0 1.9 %copy.8 = f32[768,128]{1,0:T(8,128)} copy(f32[768,128]{0,1:T(8,128)} %bitcast.8) | data formatting | bytes 786432
  37.9 1.5 %copy.11 = f32[1,4,32,128]{3,2,1,0:T(8,128)} copy(f32[1,4,32,128]{3,2,1,0:T(8,128)} %bitcast.10) | data formatting | bytes 131072
  39.4 2.3 %copy.12 = f32[1,4,512,128]{3,2,1,0:T(8,128)} copy(f32[1,4,512,128]{3,2,1,0:T(8,128)} %bitcast.7) | data formatting | bytes 2097152

commit v2 on v1

--- a/solution.py
+++ b/solution.py
@@ -21,10 +21,10 @@
 
 
 def kernel(
-    dims, lens, qhid, proj, phid, qg_out, pg_out, wg_out, loss_out,
-    tok, ptok, ptok_t, phid_v, expo, grad_a, sums, pooled, sc, lo, qsend, qrecv, pg_v, pg_t,
-    wsend, wrecv, zbuf, cbuf,
-    in_sem, out_sem, tok_s, tok_r, sc_s, sc_r, lo_s, lo_r, qg_s, qg_r, ws_s, ws_r, z_s, z_r, c_s, c_r,
+    dims, lens, qhid, proj, phid, qg_out, pg_v, cbuf, loss_out,
+    tok, ptok, ptok_t, phid_v, expo, grad_a, sums, pooled, sc, lo, qsend, qrecv,
+    wsend, wrecv, zbuf,
+    in_sem, tok_s, tok_r, sc_s, sc_r, lo_s, lo_r, qg_s, qg_r, ws_s, ws_r, z_s, z_r, c_s, c_r,
 ):
     nblk, nrep, ncore, nquery, qlen, npass, plen = dims
     ntok = nquery * qlen
@@ -153,7 +153,7 @@
 
     qg_t = lax.fori_loop(0, npass, backward, jnp.zeros((dim, nqi), F32))
     for b in range(nblk):
-        qsend[b] = qg_t[:, b * ntok : (b + 1) * ntok]
+        qsend[b] = qg_t[:, b * ntok : (b + 1) * ntok].astype(BF16)
     qrecv[blk] = qsend[blk]
     qg_copies = share(lambda k: qsend.at[lax.rem(blk + k, nblk)], qrecv.at[blk], qg_s, qg_r, blk_peer, nblk)
 
@@ -163,11 +163,9 @@
         return acc + jnp.dot(g.astype(BF16).T, phid_v[p], preferred_element_type=F32)
 
     wg_t = lax.fori_loop(0, npass, passages, jnp.zeros((dim, qhid.shape[1]), F32))
-    store = pltpu.make_async_copy(pg_v, pg_out, out_sem)
-    store.start()
     for copy in qg_copies:
         copy.wait_recv()
-    mine_t = jnp.sum(qrecv[...], 0)
+    mine_t = jnp.sum(qrecv[...].astype(F32), 0)
     wg_t = wg_t + jnp.dot(mine_t.astype(BF16), qhid[...], preferred_element_type=F32)
     depth = dim // na
     for a in range(na):
@@ -188,13 +186,25 @@
     c_copies = share(lambda k: cbuf.at[me_a], cbuf.at[me_a], c_s, c_r, a_peer, na)
     for copy in tok_copies + sc_copies + lo_copies + qg_copies + ws_copies + z_copies:
         copy.wait_send()
-    store.wait()
     for copy in c_copies:
         copy.wait_recv()
-    for a in range(na):
-        wg_out[a * depth : (a + 1) * depth, :] = cbuf[a].astype(F32)
     for copy in c_copies:
         copy.wait_send()
+
+
+def write_out(qg, pg, wg_t, loss, qg_out, pg_out, wg_out, loss_out, wg_v, sem):
+    first = pltpu.make_async_copy(pg, pg_out, sem.at[0])
+    first.start()
+    second = pltpu.make_async_copy(qg, qg_out, sem.at[1])
+    second.start()
+    na, depth, hidden = wg_t.shape
+    wg_v[...] = wg_t[...].astype(F32).reshape(na * depth, hidden).T
+    third = pltpu.make_async_copy(wg_v, wg_out, sem.at[2])
+    third.start()
+    loss_out[0, 0] = loss[0, 0]
+    first.wait()
+    second.wait()
+    third.wait()
 
 
 def shards(query_hidden, passage_hidden, lengths, projection):
@@ -216,18 +226,18 @@
     pairs = []
     for n in (nblk, nblk, nrep, nblk, na, nz, na):
         pairs += [sem(n - 1), sem(n - 1)]
-    qg, pg, wg_t, loss = pl.pallas_call(
+    held = pl.pallas_call(
         functools.partial(kernel, dims),
         out_shape=(
-            jax.ShapeDtypeStruct((ntok, dim), F32),
-            jax.ShapeDtypeStruct((npass, plen, dim), F32),
-            jax.ShapeDtypeStruct((dim, hidden), F32),
-            jax.ShapeDtypeStruct((8, 128), F32),
+            pltpu.VMEM((ntok, dim), F32),
+            pltpu.VMEM((npass, plen, dim), F32),
+            pltpu.VMEM((na, dim // na, hidden), BF16),
+            pltpu.VMEM((8, 128), F32),
         ),
         in_specs=[
             pl.BlockSpec(memory_space=pltpu.SMEM), vmem, vmem, pl.BlockSpec(memory_space=pl.ANY),
         ],
-        out_specs=(vmem, pl.BlockSpec(memory_space=pl.ANY), vmem, vmem),
+        out_specs=(vmem, vmem, vmem, vmem),
         scratch_shapes=[
             pltpu.VMEM((nblk, ntok, dim), BF16),
             pltpu.VMEM((npass, plen, dim), BF16),
@@ -239,16 +249,12 @@
             pltpu.VMEM((ppad, nqi), F32),
             pltpu.VMEM((nblk, ppad, qpad), F32),
             pltpu.VMEM((nrep, 8, 128), F32),
-            pltpu.VMEM((nblk, dim, ntok), F32),
-            pltpu.VMEM((nblk, dim, ntok), F32),
-            pltpu.VMEM((npass, plen, dim), F32),
-            pltpu.VMEM((dim, plen), BF16),
+            pltpu.VMEM((nblk, dim, ntok), BF16),
+            pltpu.VMEM((nblk, dim, ntok), BF16),
             pltpu.VMEM((na, dim // na, hidden), BF16),
             pltpu.VMEM((na, dim // na, hidden), BF16),
             pltpu.VMEM((nz, dim // na, hidden), BF16),
-            pltpu.VMEM((na, dim // na, hidden), BF16),
             sem(npass),
-            pltpu.SemaphoreType.DMA,
         ] + pairs,
         compiler_params=pltpu.CompilerParams(
             collective_id=0, has_side_effects=True, vmem_limit_bytes=56 << 20
@@ -259,11 +265,25 @@
         projection,
         passage_hidden.reshape(npass, plen, hidden),
     )
+    hbm = pl.BlockSpec(memory_space=pl.ANY)
+    qg, pg, wg, loss = pl.pallas_call(
+        write_out,
+        out_shape=(
+            jax.ShapeDtypeStruct((ntok, dim), F32),
+            jax.ShapeDtypeStruct((npass, plen, dim), F32),
+            jax.ShapeDtypeStruct((hidden, dim), F32),
+            jax.ShapeDtypeStruct((1, 1), F32),
+        ),
+        in_specs=[vmem] * 4,
+        out_specs=(hbm, hbm, hbm, pl.BlockSpec(memory_space=pltpu.SMEM)),
+        scratch_shapes=[pltpu.VMEM((hidden, dim), F32), sem(3)],
+        compiler_params=pltpu.CompilerParams(vmem_limit_bytes=8 << 20),
+    )(*[pltpu.with_memory_space_constraint(x, pltpu.VMEM) for x in held])
     return (
         qg.reshape(1, nquery, qlen, dim),
         pg.reshape(1, npass, plen, dim),
-        wg_t.T,
-        loss[0, 0],
+        wg,
+        loss.reshape(()),
     )
 
 

time: 42 us -> 35.1 us (0.84)
  local copies, waits for them, and re-layouts: 6.83 us -> 0 us
    unnamed x3 -> x0, local copies, waits for them, and re-layouts: 5.64 us -> none
    slice x1 -> x0, local copies, waits for them, and re-layouts: 1.18 us -> none  [shards(): loss[0, 0]]
    pallas_call x1 -> x2, Pallas kernels: 34.2 us -> 34.3 us  [the longest x1 32.6 us: shards(): pl.pallas_call(functools.partial(kernel, dims), out_shape=(pltpu.VMEM((nt...]
where the time goes in v2:
time: 35.1 us; the launch traced here: 34.9 us
  Pallas kernels  34.3 us (98%)
  between operations  0.64 us (2%)
    pallas_call x1, Pallas kernels, shards(): pl.pallas_call(functools.partial(kernel, dims), out_shape=(pltpu.VMEM((nt...  32.6 us
    pallas_call x1, Pallas kernels, shards(): pl.pallas_call(write_out, out_shape=(jax.ShapeDtypeStruct((ntok, dim), F3...  1.66 us

profile of v2, /device:TPU:0, one launch (start us, length us, event | category | flops | bytes accessed | tf_op | source)
XLA Modules:
  0.0 34.9 jit_solution(7890303465352115797)
XLA Ops:
  0.6 32.6 %shard_map.75 = (f32[128,128]{1,0:T(8,128)S(1)}, f32[4,512,128]{2,1,0:T(8,128)S(1)}, bf16[8,16,768]{2,1,0:T(8,128)(2,1)S(1)}, f32[8,128]{1,0:T(8,128)S(1)}) custom-call(s32[1,4]{1,0:T(1,128)} %lens.1, bf16[128,768]{1,0:T(8,128)(2,1)} %bitcast.6, bf16[768,128]{1,0:T(8,128)(2,1)} %proj.1, bf16[4,512,768]{2,1,0:T(8,128)(2,1)} %bitcast.5), custom_call_target="tpu_custom_call" | custom-call | tf_op jit(solution)/shard_map/pallas_call | solution.py:229
  33.2 1.7 %shard_map.76 = (f32[128,128]{1,0:T(8,128)}, f32[4,512,128]{2,1,0:T(8,128)}, f32[768,128]{1,0:T(8,128)}, f32[1,1]{1,0:T(1,128)}) custom-call(f32[128,128]{1,0:T(8,128)S(1)} %get-tuple-element.12.qg, f32[4,512,128]{2,1,0:T(8,128)S(1)} %get-tuple-element.13.pg, bf16[8,16,768]{2,1,0:T(8,128)(2,1)S(1)} %get-tuple-element.14.wg_t, ...), custom_call_target="tpu_custom_call" | custom-call | tf_op jit(solution)/shard_map/pallas_call | solution.py:269

commit v3 on v2

v3 whole, which is shorter than its diff:
```python
import functools

import jax
import jax.numpy as jnp
from jax import lax
from jax.experimental import pallas as pl
from jax.experimental.pallas import tpu as pltpu
from jax.sharding import PartitionSpec as P

MESH = pl.DeviceIdType.MESH
F32 = jnp.float32
BF16 = jnp.bfloat16
HIGH = lax.Precision.HIGHEST
NT = (((1,), (1,)), ((), ()))

temper = 0.5


def rows_iota(shape, dim):
    return lax.broadcasted_iota(jnp.int32, shape, dim)


def kernel(
    dims, lens_in, qhid_in, proj_in, phid_in, qg_out, pg_out, cbuf, loss_out,
    lens, qhid, proj, phid, tok, ptok, ptok_t, expo, grad_a, sums, tops, sc, lo, qsend, qrecv,
    wsend, wrecv, zbuf,
    in_sem, tok_s, tok_r, sc_s, sc_r, lo_s, lo_r, qg_s, qg_r, ws_s, ws_r, z_s, z_r, c_s, c_r,
):
    nblk, nrep, ncore, ncol, nquery, qlen, npass, plen = dims
    ntok = nquery * qlen
    nqi = nblk * ntok
    nq_all = nblk * nquery
    nz = nrep // ncore
    na = nblk * ncore
    nrow = nblk // ncol
    hidden, dim = proj.shape
    total = nq_all * nrep
    blk = lax.axis_index("blk")
    rep = lax.axis_index("rep")
    core = lax.rem(rep, ncore)
    zed = rep // ncore
    me_a = blk * ncore + core

    def blk_index(k):
        high = lax.rem(blk // ncol + k // ncol, nrow)
        low = lax.rem(lax.rem(blk, ncol) + k % ncol, ncol)
        return high * ncol + low

    def opposite(k):
        return (nrow - k // ncol) % nrow * ncol + (ncol - k % ncol) % ncol

    def blk_peer(k):
        return (blk_index(k), rep)

    def rep_peer(k):
        return (blk, lax.rem(rep + k, nrep))

    def a_index(k):
        return lax.rem(me_a + k, na)

    def a_peer(k):
        other = a_index(k)
        return (other // ncore, zed * ncore + lax.rem(other, ncore))

    def z_peer(k):
        return (blk, lax.rem(zed + k, nz) * ncore + core)

    def send(src, dst, send_sem, recv_sem, peer):
        copy = pltpu.make_async_remote_copy(
            src_ref=src, dst_ref=dst, send_sem=send_sem, recv_sem=recv_sem,
            device_id=peer, device_id_type=MESH,
        )
        copy.start()
        return copy

    def share(src, dst, send_sem, recv_sem, peer, count):
        return [
            send(src(k), dst, send_sem.at[k - 1], recv_sem.at[k - 1], peer(k)) for k in range(1, count)
        ]

    barrier = pltpu.get_barrier_semaphore()
    greeted = 0
    for count, peer in ((nrep, rep_peer), (na, a_peer)):
        for k in range(1, count):
            pl.semaphore_signal(barrier, inc=1, device_id=peer(k), device_id_type=MESH)
            greeted += 1

    loads = []
    pairs = [(qhid_in, qhid), (proj_in, proj), (lens_in, lens)]
    pairs += [(phid_in.at[p], phid.at[p]) for p in range(npass)]
    for n, (src, dst) in enumerate(pairs):
        load = pltpu.make_async_copy(src, dst, in_sem.at[n])
        load.start()
        loads.append(load)

    sums[...] = jnp.ones_like(sums)
    tops[...] = jnp.zeros_like(tops)
    loads[0].wait()
    loads[1].wait()
    tok[0] = jnp.dot(qhid[...], proj[...], preferred_element_type=F32).astype(BF16)
    pl.semaphore_wait(barrier, greeted)
    far = list(range(nblk - 1, 0, -1))
    tok_copies = {
        k: send(tok.at[0], tok.at[opposite(k)], tok_s.at[k - 1], tok_r.at[k - 1], blk_peer(k)) for k in far
    }

    loads[2].wait()
    ppad = sums.shape[1]
    qpad = sc.shape[2]
    size = jnp.ones((ppad, ntok), jnp.int32)
    for p in range(npass):
        size = jnp.where(rows_iota(size.shape, 0) == p, lens[0, p], size)
    log_size = jnp.log(size.astype(F32))
    for p in range(npass):
        loads[3 + p].wait()
        vec = jnp.dot(phid[p], proj[...], preferred_element_type=F32).astype(BF16)
        ptok[p] = vec
        ptok_t[p] = vec.T

    def forward(k):
        token = tok[k]

        def step(p, carry):
            a = lax.dot_general(ptok[p], token, NT, preferred_element_type=F32)
            valid = rows_iota(a.shape, 0) < lens[0, p]
            scaled = jnp.where(valid, a / temper, -jnp.inf)
            top = jnp.max(scaled, 0, keepdims=True)
            e = jnp.exp(scaled - top)
            expo[k, p] = e
            sums[k, pl.ds(p, 1), :] = jnp.sum(e, 0, keepdims=True)
            tops[k, pl.ds(p, 1), :] = top
            return carry

        lax.fori_loop(0, npass, step, 0)
        pooled = temper * (tops[k] + jnp.log(sums[k]) - log_size)
        query = rows_iota((ntok, qpad), 1) - blk_index(k) * nquery
        place = rows_iota((ntok, qpad), 0)
        pick = ((place >= query * qlen) & (place < (query + 1) * qlen)).astype(F32)
        return jnp.dot(pooled, pick, precision=HIGH, preferred_element_type=F32)

    own = forward(0)
    for k in range(1, nblk):
        tok_copies[opposite(k)].wait_recv()
        own = own + forward(k)
    sc[blk] = own
    sc_copies = [
        send(sc.at[blk], sc.at[blk], sc_s.at[k - 1], sc_r.at[k - 1], blk_peer(k)) for k in far
    ]
    for copy in sc_copies:
        copy.wait_recv()

    score = sc[...]
    row = rows_iota(score.shape, 1)
    lane = rows_iota(score.shape, 2)
    slot = rows_iota(score.shape, 0)
    live = row < npass
    hidden_score = jnp.where(live, score, -jnp.inf)
    top = jnp.max(jnp.max(hidden_score, 0), 0, keepdims=True)
    lse = top + jnp.log(jnp.sum(jnp.sum(jnp.exp(hidden_score - top[None]), 0), 0, keepdims=True))
    mine = rows_iota(own.shape, 0) + blk * npass == rows_iota(own.shape, 1)
    dscore = (jnp.exp(own - lse) - mine.astype(F32)) / total

    def backward(k):
        query = rows_iota((qpad, ntok), 0) - blk_index(k) * nquery
        place = rows_iota((qpad, ntok), 1)
        spread = ((place >= query * qlen) & (place < (query + 1) * qlen)).astype(F32)
        sums[k] = jnp.dot(dscore, spread, precision=HIGH, preferred_element_type=F32) / sums[k]

        def step(p, acc):
            d = (expo[k, p] * sums[k, pl.ds(p, 1), :]).astype(BF16)
            grad_a[p, :, k * ntok : (k + 1) * ntok] = d
            return acc + jnp.dot(ptok_t[p], d, preferred_element_type=F32)

        return lax.fori_loop(0, npass, step, jnp.zeros((dim, ntok), F32))

    qg_copies = []
    for k in far:
        qsend[k] = backward(k).astype(BF16)
        qg_copies.append(
            send(qsend.at[k], qrecv.at[opposite(k)], qg_s.at[k - 1], qg_r.at[k - 1], blk_peer(k))
        )
    mine_t = backward(0)

    hit = live & (slot * npass + row == lane)
    aim = jnp.sum(jnp.sum(jnp.where(hit, score, 0.0), 0), 0, keepdims=True)
    gap = jnp.where(rows_iota(lse.shape, 1) < nq_all, lse - aim, 0.0)
    part = jnp.sum(gap, 1, keepdims=True)
    lo[rep] = jnp.broadcast_to(part, lo.shape[1:])
    lo_copies = share(lambda k: lo.at[rep], lo.at[rep], lo_s, lo_r, rep_peer, nrep)

    every = tok[...].reshape(nqi, dim)

    def passages(p, acc):
        g = jnp.dot(grad_a[p], every, preferred_element_type=F32)
        pg_out[p] = g
        return acc + jnp.dot(g.astype(BF16).T, phid[p], preferred_element_type=F32)

    wg_t = lax.fori_loop(0, npass, passages, jnp.zeros((dim, hidden), F32))
    for copy in qg_copies:
        copy.wait_recv()
    for k in range(1, nblk):
        mine_t = mine_t + qrecv[k].astype(F32)
    wg_t = wg_t + jnp.dot(mine_t.astype(BF16), qhid[...], preferred_element_type=F32)
    depth = dim // na
    halves = range(wsend.shape[0])
    width = wsend.shape[3]
    ws_copies = []
    for h in halves:
        for a in range(na):
            wsend[h, a] = wg_t[a * depth : (a + 1) * depth, h * width : (h + 1) * width].astype(BF16)
        wrecv[h, me_a] = wsend[h, me_a]
        ws_copies.append(
            share(
                lambda k: wsend.at[h, a_index(k)], wrecv.at[h, me_a], ws_s.at[h], ws_r.at[h], a_peer, na
            )
        )
    qg_out[...] = mine_t.T
    z_copies = []
    for h in halves:
        for copy in ws_copies[h]:
            copy.wait_recv()
        zbuf[h, zed] = jnp.sum(wrecv[h].astype(F32), 0).astype(BF16)
        z_copies.append(
            share(lambda k: zbuf.at[h, zed], zbuf.at[h, zed], z_s.at[h], z_r.at[h], z_peer, nz)
        )
    for copy in lo_copies:
        copy.wait_recv()
    loss_out[...] = jnp.sum(lo[...], 0) / total
    c_copies = []
    for h in halves:
        for copy in z_copies[h]:
            copy.wait_recv()
        cbuf[h, me_a] = jnp.sum(zbuf[h].astype(F32), 0).astype(BF16)
        c_copies.append(
            share(lambda k: cbuf.at[h, me_a], cbuf.at[h, me_a], c_s.at[h], c_r.at[h], a_peer, na)
        )
    for copy in list(tok_copies.values()) + sc_copies + lo_copies + qg_copies:
        copy.wait_send()
    for h in halves:
        for copy in ws_copies[h] + z_copies[h]:
            copy.wait_send()
    for h in halves:
        for copy in c_copies[h]:
            copy.wait()


def write_out(qg, pg, wg_t, loss, qg_out, pg_out, wg_out, loss_out, wg_v, sem):
    copies = [pltpu.make_async_copy(pg.at[p], pg_out.at[p], sem.at[p]) for p in range(pg.shape[0])]
    copies.append(pltpu.make_async_copy(qg, qg_out, sem.at[pg.shape[0]]))
    for copy in copies:
        copy.start()
    nhalf, na, depth, width = wg_t.shape
    for h in range(nhalf):
        rows = slice(h * width, (h + 1) * width)
        wg_v[rows, :] = wg_t[h].astype(F32).reshape(na * depth, width).T
        copy = pltpu.make_async_copy(wg_v.at[rows], wg_out.at[rows], sem.at[pg.shape[0] + 1 + h])
        copy.start()
        copies.append(copy)
    loss_out[0, 0] = loss[0, 0]
    for copy in copies:
        copy.wait()


def shards(query_hidden, passage_hidden, lengths, projection):
    hidden, dim = projection.shape
    nquery, qlen = query_hidden.shape[1:3]
    npass, plen = passage_hidden.shape[1:3]
    nblk = lax.axis_size("blk")
    nrep = lax.axis_size("rep")
    ncore = 2 if nrep % 2 == 0 else 1
    ncol = 2 if nblk % 2 == 0 else 1
    nhalf = 2 if hidden % 256 == 0 else 1
    nz = nrep // ncore
    na = nblk * ncore
    ntok = nquery * qlen
    nqi = nblk * ntok
    ppad = -(-npass // 8) * 8
    qpad = -(-nblk * nquery // 128) * 128
    dims = (nblk, nrep, ncore, ncol, nquery, qlen, npass, plen)
    vmem = pl.BlockSpec(memory_space=pltpu.VMEM)
    hbm = pl.BlockSpec(memory_space=pl.ANY)
    piece = (dim // na, hidden // nhalf)
    sem = lambda *n: pltpu.SemaphoreType.DMA(n)
    pairs = []
    for n in (nblk, nblk, nrep, nblk):
        pairs += [sem(max(n - 1, 1)), sem(max(n - 1, 1))]
    for n in (na, nz, na):
        pairs += [sem(nhalf, max(n - 1, 1)), sem(nhalf, max(n - 1, 1))]
    held = pl.pallas_call(
        functools.partial(kernel, dims),
        out_shape=(
            pltpu.VMEM((ntok, dim), F32),
            pltpu.VMEM((npass, plen, dim), F32),
            pltpu.VMEM((nhalf, na) + piece, BF16),
            pltpu.VMEM((8, 128), F32),
        ),
        in_specs=[hbm] * 4,
        out_specs=(vmem, vmem, vmem, vmem),
        scratch_shapes=[
            pltpu.SMEM((1, npass), jnp.int32),
            pltpu.VMEM((ntok, hidden), BF16),
            pltpu.VMEM((hidden, dim), BF16),
            pltpu.VMEM((npass, plen, hidden), BF16),
            pltpu.VMEM((nblk, ntok, dim), BF16),
            pltpu.VMEM((npass, plen, dim), BF16),
            pltpu.VMEM((npass, dim, plen), BF16),
            pltpu.VMEM((nblk, npass, plen, ntok), F32),
            pltpu.VMEM((npass, plen, nqi), BF16),
            pltpu.VMEM((nblk, ppad, ntok), F32),
            pltpu.VMEM((nblk, ppad, ntok), F32),
            pltpu.VMEM((nblk, ppad, qpad), F32),
            pltpu.VMEM((nrep, 8, 128), F32),
            pltpu.VMEM((nblk, dim, ntok), BF16),
            pltpu.VMEM((nblk, dim, ntok), BF16),
            pltpu.VMEM((nhalf, na) + piece, BF16),
            pltpu.VMEM((nhalf, na) + piece, BF16),
            pltpu.VMEM((nhalf, nz) + piece, BF16),
            sem(npass + 3),
        ] + pairs,
        compiler_params=pltpu.CompilerParams(
            collective_id=0, has_side_effects=True, vmem_limit_bytes=56 << 20
        ),
    )(
        lengths,
        query_hidden.reshape(ntok, hidden),
        projection,
        passage_hidden.reshape(npass, plen, hidden),
    )
    qg, pg, wg, loss = pl.pallas_call(
        write_out,
        out_shape=(
            jax.ShapeDtypeStruct((ntok, dim), F32),
            jax.ShapeDtypeStruct((npass, plen, dim), F32),
            jax.ShapeDtypeStruct((hidden, dim), F32),
            jax.ShapeDtypeStruct((1, 1), F32),
        ),
        in_specs=[vmem] * 4,
        out_specs=(hbm, hbm, hbm, pl.BlockSpec(memory_space=pltpu.SMEM)),
        scratch_shapes=[pltpu.VMEM((hidden, dim), F32), sem(npass + 1 + nhalf)],
        compiler_params=pltpu.CompilerParams(vmem_limit_bytes=8 << 20),
    )(*[pltpu.with_memory_space_constraint(x, pltpu.VMEM) for x in held])
    return (
        qg.reshape(1, nquery, qlen, dim),
        pg.reshape(1, npass, plen, dim),
        wg,
        loss.reshape(()),
    )


def solution(mesh):
    return jax.shard_map(
        shards,
        mesh=mesh,
        in_specs=(P("rep", "blk", None, None), P("rep", "blk", None, None), P("rep", "blk"), P()),
        out_specs=(P("rep", "blk", None, None), P("rep", "blk", None, None), P(), P()),
        check_vma=False,
    )
```

time: 35.1 us -> 38 us (1.083)
  Pallas kernels: 34.3 us -> 37.2 us
    pallas_call x1, Pallas kernels: 32.6 us -> 35.5 us  [shards(): pl.pallas_call(functools.partial(kernel, dims), out_shape=(pltpu.VMEM((nt...]
where the time goes in v3:
time: 38 us; the launch traced here: 37.8 us
  Pallas kernels  37.2 us (98%)
  between operations  0.64 us (2%)
    pallas_call x1, Pallas kernels, shards(): pl.pallas_call(functools.partial(kernel, dims), out_shape=(pltpu.VMEM((nt...  35.5 us
    pallas_call x1, Pallas kernels, shards(): pl.pallas_call(write_out, out_shape=(jax.ShapeDtypeStruct((ntok, dim), F3...  1.69 us

profile of v3, /device:TPU:0, one launch (start us, length us, event | category | flops | bytes accessed | tf_op | source)
XLA Modules:
  0.0 37.8 jit_solution(14539595797833995939)
XLA Ops:
  0.6 35.5 %shard_map.75 = (f32[128,128]{1,0:T(8,128)S(1)}, f32[4,512,128]{2,1,0:T(8,128)S(1)}, bf16[2,8,16,384]{3,2,1,0:T(8,128)(2,1)S(1)}, f32[8,128]{1,0:T(8,128)S(1)}) custom-call(s32[1,4]{1,0:T(1,128)} %lens_in.1, bf16[128,768]{1,0:T(8,128)(2,1)} %bitcast.6, bf16[768,128]{1,0:T(8,128)(2,1)} %proj_in.1, bf16[4,512,768]{2,1,0:T(8,128)(2,1)} %bitcast.5), custom_call_target="tpu_custom_call" | custom-call | tf_op jit(solution)/shard_map/pallas_call | solution.py:289
  36.2 1.7 %shard_map.76 = (f32[128,128]{1,0:T(8,128)}, f32[4,512,128]{2,1,0:T(8,128)}, f32[768,128]{1,0:T(8,128)}, f32[1,1]{1,0:T(1,128)}) custom-call(f32[128,128]{1,0:T(8,128)S(1)} %get-tuple-element.12.qg, f32[4,512,128]{2,1,0:T(8,128)S(1)} %get-tuple-element.13.pg, bf16[2,8,16,384]{3,2,1,0:T(8,128)(2,1)S(1)} %get-tuple-element.14.wg_t, ...), custom_call_target="tpu_custom_call" | custom-call | tf_op jit(solution)/shard_map/pallas_call | solution.py:329

commit v4 on v2

--- a/solution.py
+++ b/solution.py
@@ -10,7 +10,6 @@
 MESH = pl.DeviceIdType.MESH
 F32 = jnp.float32
 BF16 = jnp.bfloat16
-HIGH = lax.Precision.HIGHEST
 NT = (((1,), (1,)), ((), ()))
 
 temper = 0.5
@@ -20,9 +19,18 @@
     return lax.broadcasted_iota(jnp.int32, shape, dim)
 
 
+def exact_dot(x, ones):
+    high = x.astype(BF16)
+    rest = x - high.astype(F32)
+    mid = rest.astype(BF16)
+    low = (rest - mid.astype(F32)).astype(BF16)
+    dot = lambda y: jnp.dot(y, ones, preferred_element_type=F32)
+    return dot(high) + (dot(mid) + dot(low))
+
+
 def kernel(
-    dims, lens, qhid, proj, phid, qg_out, pg_v, cbuf, loss_out,
-    tok, ptok, ptok_t, phid_v, expo, grad_a, sums, pooled, sc, lo, qsend, qrecv,
+    dims, lens_in, qhid_in, proj_in, phid, qg_out, pg_v, cbuf, loss_out,
+    lens, qhid, proj, pick, spread, tok, ptok, ptok_t, phid_v, expo, grad_a, sums, pooled, sc, lo, qsend, qrecv,
     wsend, wrecv, zbuf,
     in_sem, tok_s, tok_r, sc_s, sc_r, lo_s, lo_r, qg_s, qg_r, ws_s, ws_r, z_s, z_r, c_s, c_r,
 ):
@@ -67,12 +75,6 @@
             copies.append(copy)
         return copies
 
-    loads = []
-    for p in range(npass):
-        load = pltpu.make_async_copy(phid.at[p], phid_v.at[p], in_sem.at[p])
-        load.start()
-        loads.append(load)
-
     barrier = pltpu.get_barrier_semaphore()
     greeted = 0
     for count, peer in ((na, a_peer), (nrep, rep_peer)):
@@ -80,14 +82,31 @@
             pl.semaphore_signal(barrier, inc=1, device_id=peer(k), device_id_type=MESH)
             greeted += 1
 
+    loads = []
+    pairs = [(qhid_in, qhid), (proj_in, proj), (lens_in, lens)]
+    pairs += [(phid.at[p], phid_v.at[p]) for p in range(npass)]
+    for n, (src, dst) in enumerate(pairs):
+        load = pltpu.make_async_copy(src, dst, in_sem.at[n])
+        load.start()
+        loads.append(load)
+    qpad = sc.shape[2]
+    owner = rows_iota((nqi, qpad), 1) * qlen
+    token = rows_iota((nqi, qpad), 0)
+    pick[...] = jnp.where((token >= owner) & (token < owner + qlen), 1.0, 0.0).astype(BF16)
+    owner_t = rows_iota((qpad, nqi), 0) * qlen
+    token_t = rows_iota((qpad, nqi), 1)
+    spread[...] = jnp.where((token_t >= owner_t) & (token_t < owner_t + qlen), 1.0, 0.0).astype(BF16)
+    pooled[...] = jnp.zeros_like(pooled)
+    sums[...] = jnp.ones_like(sums)
+    loads[0].wait()
+    loads[1].wait()
     tok[blk] = jnp.dot(qhid[...], proj[...], preferred_element_type=F32).astype(BF16)
     pl.semaphore_wait(barrier, greeted)
     tok_copies = share(lambda k: tok.at[blk], tok.at[blk], tok_s, tok_r, blk_peer, nblk)
 
-    pooled[...] = jnp.zeros_like(pooled)
-    sums[...] = jnp.ones_like(sums)
+    loads[2].wait()
     for p in range(npass):
-        loads[p].wait()
+        loads[3 + p].wait()
         vec = jnp.dot(phid_v[p], proj[...], preferred_element_type=F32).astype(BF16)
         ptok[p] = vec
         ptok_t[p] = vec.T
@@ -111,17 +130,9 @@
 
     lax.fori_loop(0, npass, forward, 0)
 
-    ppad = pooled.shape[0]
-    qpad = sc.shape[2]
-    owner = rows_iota((nqi, qpad), 1) * qlen
-    token = rows_iota((nqi, qpad), 0)
-    pick = ((token >= owner) & (token < owner + qlen)).astype(F32)
-    own = jnp.dot(pooled[...], pick, precision=HIGH, preferred_element_type=F32)
+    own = exact_dot(pooled[...], pick[...])
     sc[blk] = own
     sc_copies = share(lambda k: sc.at[blk], sc.at[blk], sc_s, sc_r, blk_peer, nblk)
-    owner_t = rows_iota((qpad, nqi), 0) * qlen
-    token_t = rows_iota((qpad, nqi), 1)
-    spread = ((token_t >= owner_t) & (token_t < owner_t + qlen)).astype(F32)
     inv = 1.0 / sums[...]
     for copy in sc_copies:
         copy.wait_recv()
@@ -134,6 +145,22 @@
     hidden_score = jnp.where(live, score, -jnp.inf)
     top = jnp.max(jnp.max(hidden_score, 0), 0, keepdims=True)
     lse = top + jnp.log(jnp.sum(jnp.sum(jnp.exp(hidden_score - top[None]), 0), 0, keepdims=True))
+    mine = rows_iota(own.shape, 0) + blk * npass == rows_iota(own.shape, 1)
+    dscore = (jnp.exp(own - lse) - mine.astype(F32)) / total
+    factor = exact_dot(dscore, spread[...]) * inv
+    sums[...] = factor
+
+    def backward(p, acc):
+        d = (expo[p] * sums[pl.ds(p, 1), :]).astype(BF16)
+        grad_a[p] = d
+        return acc + jnp.dot(ptok_t[p], d, preferred_element_type=F32)
+
+    qg_t = lax.fori_loop(0, npass, backward, jnp.zeros((dim, nqi), F32))
+    for b in range(nblk):
+        qsend[b] = qg_t[:, b * ntok : (b + 1) * ntok].astype(BF16)
+    qrecv[blk] = qsend[blk]
+    qg_copies = share(lambda k: qsend.at[lax.rem(blk + k, nblk)], qrecv.at[blk], qg_s, qg_r, blk_peer, nblk)
+
     hit = live & (slot * npass + row == lane)
     aim = jnp.sum(jnp.sum(jnp.where(hit, score, 0.0), 0), 0, keepdims=True)
     gap = jnp.where(rows_iota(lse.shape, 1) < nq_all, lse - aim, 0.0)
@@ -141,21 +168,6 @@
     lo[rep] = jnp.broadcast_to(part, lo.shape[1:])
     lo_copies = share(lambda k: lo.at[rep], lo.at[rep], lo_s, lo_r, rep_peer, nrep)
 
-    mine = rows_iota(own.shape, 0) + blk * npass == rows_iota(own.shape, 1)
-    dscore = (jnp.exp(own - lse) - mine.astype(F32)) / total
-    factor = jnp.dot(dscore, spread, precision=HIGH, preferred_element_type=F32) * inv
-    sums[...] = factor
-
-    def backward(p, acc):
-        d = (expo[p] * sums[pl.ds(p, 1), :]).astype(BF16)
-        grad_a[p] = d
-        return acc + jnp.dot(ptok_t[p], d, preferred_element_type=F32)
-
-    qg_t = lax.fori_loop(0, npass, backward, jnp.zeros((dim, nqi), F32))
-    for b in range(nblk):
-        qsend[b] = qg_t[:, b * ntok : (b + 1) * ntok].astype(BF16)
-    qrecv[blk] = qsend[blk]
-    qg_copies = share(lambda k: qsend.at[lax.rem(blk + k, nblk)], qrecv.at[blk], qg_s, qg_r, blk_peer, nblk)
 
     def passages(p, acc):
         g = jnp.dot(grad_a[p], every, preferred_element_type=F32)
@@ -235,10 +247,15 @@
             pltpu.VMEM((8, 128), F32),
         ),
         in_specs=[
-            pl.BlockSpec(memory_space=pltpu.SMEM), vmem, vmem, pl.BlockSpec(memory_space=pl.ANY),
+            *[pl.BlockSpec(memory_space=pl.ANY)] * 4,
         ],
         out_specs=(vmem, vmem, vmem, vmem),
         scratch_shapes=[
+            pltpu.SMEM((1, npass), jnp.int32),
+            pltpu.VMEM((ntok, hidden), BF16),
+            pltpu.VMEM((hidden, dim), BF16),
+            pltpu.VMEM((nqi, qpad), BF16),
+            pltpu.VMEM((qpad, nqi), BF16),
             pltpu.VMEM((nblk, ntok, dim), BF16),
             pltpu.VMEM((npass, plen, dim), BF16),
             pltpu.VMEM((npass, dim, plen), BF16),
@@ -254,7 +271,7 @@
             pltpu.VMEM((na, dim // na, hidden), BF16),
             pltpu.VMEM((na, dim // na, hidden), BF16),
             pltpu.VMEM((nz, dim // na, hidden), BF16),
-            sem(npass),
+            sem(npass + 3),
         ] + pairs,
         compiler_params=pltpu.CompilerParams(
             collective_id=0, has_side_effects=True, vmem_limit_bytes=56 << 20

time: 35.1 us -> 33.8 us (0.963)
  Pallas kernels: 34.3 us -> 33 us
    pallas_call x1, Pallas kernels: 32.6 us -> 31.4 us  [shards(): pl.pallas_call(functools.partial(kernel, dims), out_shape=(pltpu.VMEM((nt...]
where the time goes in v4:
time: 33.8 us; the launch traced here: 33.7 us
  Pallas kernels  33 us (98%)
  between operations  0.64 us (2%)
    pallas_call x1, Pallas kernels, shards(): pl.pallas_call(functools.partial(kernel, dims), out_shape=(pltpu.VMEM((nt...  31.4 us
    pallas_call x1, Pallas kernels, shards(): pl.pallas_call(write_out, out_shape=(jax.ShapeDtypeStruct((ntok, dim), F3...  1.66 us

profile of v4, /device:TPU:0, one launch (start us, length us, event | category | flops | bytes accessed | tf_op | source)
XLA Modules:
  0.0 33.7 jit_solution(13045647137931959421)
XLA Ops:
  0.6 31.4 %shard_map.75 = (f32[128,128]{1,0:T(8,128)S(1)}, f32[4,512,128]{2,1,0:T(8,128)S(1)}, bf16[8,16,768]{2,1,0:T(8,128)(2,1)S(1)}, f32[8,128]{1,0:T(8,128)S(1)}) custom-call(s32[1,4]{1,0:T(1,128)} %lens_in.1, bf16[128,768]{1,0:T(8,128)(2,1)} %bitcast.6, bf16[768,128]{1,0:T(8,128)(2,1)} %proj_in.1, bf16[4,512,768]{2,1,0:T(8,128)(2,1)} %bitcast.5), custom_call_target="tpu_custom_call" | custom-call | tf_op jit(solution)/shard_map/pallas_call | solution.py:241
  32.0 1.7 %shard_map.76 = (f32[128,128]{1,0:T(8,128)}, f32[4,512,128]{2,1,0:T(8,128)}, f32[768,128]{1,0:T(8,128)}, f32[1,1]{1,0:T(1,128)}) custom-call(f32[128,128]{1,0:T(8,128)S(1)} %get-tuple-element.12.qg, f32[4,512,128]{2,1,0:T(8,128)S(1)} %get-tuple-element.13.pg, bf16[8,16,768]{2,1,0:T(8,128)(2,1)S(1)} %get-tuple-element.14.wg_t, ...), custom_call_target="tpu_custom_call" | custom-call | tf_op jit(solution)/shard_map/pallas_call | solution.py:286
